TPU v7x, 32 devices: a whole 2x2x4 slice. The times are simulated.
32 devices in a mesh: dp: 8 (over z, y), tensor: 4 (over x, core).
Axes of the slice: x: 2, y: 2, z: 4, core: 2. Of those that a mesh axis runs over, the one named last changes fastest.
Arguments:
- layer_input: bfloat16 [4096, 16384], P('dp', 'tensor'), may hold values from -6 to 6
- queries: bfloat16 [4096, 4096], P('dp', 'tensor'), may hold values from -128 to 128
- key_value: bfloat16 [4096, 512], P('dp', 'tensor'), may hold values from -16 to 16
- out_grad: bfloat16 [4096, 4096], P('dp', 'tensor'), may hold values from -6 to 6
- segment_ids: int32 [8, 512], P('dp'), may hold values from 0 to 63, as said below
Outputs:
- grad_query: bfloat16 [4096, 4096], P('dp', 'tensor')
- grad_key_value: bfloat16 [4096, 512], P('dp', 'tensor')
- grad_weights: bfloat16 [16384, 512], P(('tensor', 'dp'))
Inputs may be any that keep to these rules, and one draw needn't show every extreme that they name: `segment_ids`: along each sequence the ids start at 0, never fall, and rise by one at most, only at positions that are multiples of 8.
All inputs are finite; a program needn't handle non-finite values.
Results may differ from a plain program's by a relative error of at most 0.017.
Values may be sent and summed in bfloat16 or wider, within the bound.
A program may use at most 128 MiB of HBM per device.

v0:
```python
import jax
import jax.numpy as jnp
from jax import lax
from jax.sharding import PartitionSpec as P


def partner_2(value, axis, stride):
    mask = 2**stride
    pairs = [(source, source ^ mask) for source in range(lax.axis_size(axis))]
    return lax.ppermute(value, axis, pairs)


def score_block(query_block, grad_block, key_rows, value_rows, allowed, score_scale):
    scores = (
        jnp.einsum("thd,sd->hts", query_block, key_rows, preferred_element_type=jnp.float32)
        * score_scale
    )
    scores = jnp.where(allowed[None], scores, -1e30)
    row_max = jnp.max(scores, axis=-1, keepdims=True)
    weights = jnp.exp(scores - row_max)
    probability = weights / jnp.sum(weights, axis=-1, keepdims=True)
    prob_rounded = probability.astype(jnp.bfloat16)
    attended = jnp.einsum(
        "hts,sd->thd", prob_rounded, value_rows, preferred_element_type=jnp.float32
    )
    row_delta = jnp.sum(grad_block.astype(jnp.float32) * attended, axis=-1)
    prob_grad = jnp.einsum(
        "thd,sd->hts", grad_block, value_rows, preferred_element_type=jnp.float32
    )
    score_rounded = (probability * (prob_grad - row_delta.T[:, :, None])).astype(jnp.bfloat16)
    key_term = (
        jnp.einsum("hts,thd->sd", score_rounded, query_block, preferred_element_type=jnp.float32)
        * score_scale
    )
    value_term = jnp.einsum(
        "hts,thd->sd", prob_rounded, grad_block, preferred_element_type=jnp.float32
    )
    return (score_rounded, key_term, value_term)


def shards(layer_input, queries, key_value, out_grad, segment_ids):
    tok_rows = queries.shape[0]
    head_width = key_value.shape[1]
    group_count = queries.shape[1] // head_width // 2
    score_scale = head_width ** (-0.5)
    partner = partner_2(key_value, "tensor", 0)
    is_even = lax.axis_index("tensor") % 2 == 0
    key_rows = jnp.where(is_even, key_value, partner)
    value_rows = jnp.where(is_even, partner, key_value)
    position = jnp.arange(tok_rows)
    segment_row = segment_ids[0]
    allowed = (position[None, :] <= position[:, None]) & (
        segment_row[:, None] == segment_row[None, :]
    )
    query_blocks = queries.reshape(tok_rows, group_count, 2, head_width)
    grad_blocks = out_grad.reshape(tok_rows, group_count, 2, head_width)
    zero_grad = jnp.zeros((tok_rows, head_width), jnp.float32)

    def block_terms(block_index):
        query_block = lax.dynamic_index_in_dim(query_blocks, block_index, 1, keepdims=False)
        grad_block = lax.dynamic_index_in_dim(grad_blocks, block_index, 1, keepdims=False)
        return score_block(query_block, grad_block, key_rows, value_rows, allowed, score_scale)

    def stored_step(block_index, state_carry):
        score_buffer, key_grad, value_grad = state_carry
        score_rounded, key_term, value_term = block_terms(block_index)
        score_buffer = lax.dynamic_update_index_in_dim(score_buffer, score_rounded, block_index, 0)
        return (score_buffer, key_grad + key_term, value_grad + value_term)

    score_buffer, key_grad, value_grad = lax.fori_loop(
        0,
        group_count,
        stored_step,
        (jnp.zeros((group_count, 2, tok_rows, tok_rows), jnp.bfloat16), zero_grad, zero_grad),
    )
    tensor_count = lax.axis_size("tensor")
    stacked = jnp.concatenate([key_grad, value_grad], axis=1)
    every_part = lax.all_gather(stacked.astype(jnp.bfloat16), "tensor", axis=1, tiled=True).astype(
        stacked.dtype
    )
    summed_pairs = every_part.reshape(tok_rows, tensor_count // 2, 2, 2, head_width).sum(axis=2)
    all_grads = summed_pairs.astype(jnp.bfloat16).reshape(tok_rows, tensor_count * head_width)
    grad_pair = lax.dynamic_slice_in_dim(
        all_grads, lax.axis_index("tensor") * head_width, head_width, 1
    )
    query_full = (
        jnp.einsum("ghts,sd->tghd", score_buffer, key_rows, preferred_element_type=jnp.float32)
        * score_scale
    )
    grad_query = query_full.astype(jnp.bfloat16).reshape(tok_rows, queries.shape[1])
    sequences = lax.axis_size("dp")
    product = lax.dot_general(
        layer_input, all_grads, (((0,), (0,)), ((), ())), preferred_element_type=jnp.float32
    )
    weight_grad = lax.psum_scatter(
        (product / sequences).astype(jnp.bfloat16), "dp", scatter_dimension=0, tiled=True
    )
    return (grad_query, grad_pair, weight_grad)


def solution(mesh):
    return jax.shard_map(
        shards,
        mesh=mesh,
        in_specs=(
            P("dp", "tensor"),
            P("dp", "tensor"),
            P("dp", "tensor"),
            P("dp", "tensor"),
            P("dp", None),
        ),
        out_specs=(P("dp", "tensor"), P("dp", "tensor"), P(("tensor", "dp"), None)),
        check_vma=False,
    )
```

profile of v0, /device:TPU:0, one launch (start us, length us, event | category | flops | bytes accessed | tf_op | source)
XLA Modules:
  0.0 162.0 jit_solution(8521090285912653832)
XLA Ops:
  7.2 0.0 all-gather.2.cloned.1.call-start
  7.2 1.0 copy.24
  8.2 0.5 collective-permute-start
  8.7 0.0 copy-start
  8.7 1.5 copy.25
  10.3 1.5 copy.26
  11.8 0.0 collective-permute-done
  11.8 0.1 copy.29
  11.9 0.0 copy-done
  11.9 21.7 %while.18 = (s32[]{:T(128)}, bf16[4,2,512,512]{2,3,1,0:T(8,128)(2,1)}, f32[512,128]{1,0:T(8,128)S(1)}, f32[512,128]{1,0:T(8,128)S(1)}, bf16[512,4,2,128]{0,3,2,1...) while((s32[]{:T(128)}, ...), condition=%wide.region_4.5_spmd.clone, body=%wide.region_0.4_spmd.clone.sunk | while | flops 678886912 | bytes 21125260 | solution.py:70
  12.0 0.2 copy.44
  12.2 0.2 fusion.66
  12.4 0.4 fusion.65
  12.8 1.2 fusion.67
  14.0 0.3 fusion.68
  14.3 0.6 fusion.69
  14.9 0.5 fusion.71
  15.4 1.5 bitcast_dynamic-update-slice_fusion.2
  16.9 0.5 fusion.70
  17.4 0.2 copy.44
  17.6 0.2 fusion.66
  17.8 0.4 fusion.65
  18.2 1.2 fusion.67
  19.4 0.3 fusion.68
  19.7 0.6 fusion.69
  20.3 0.5 fusion.71
  20.8 1.5 bitcast_dynamic-update-slice_fusion.2
  22.3 0.5 fusion.70
  22.8 0.2 copy.44
  23.0 0.2 fusion.66
  23.2 0.4 fusion.65
  23.7 1.2 fusion.67
  24.9 0.3 fusion.68
  25.2 0.6 fusion.69
  25.7 0.5 fusion.71
  26.2 1.5 bitcast_dynamic-update-slice_fusion.2
  27.7 0.5 fusion.70
  28.3 0.2 copy.44
  28.5 0.2 fusion.66
  28.7 0.4 fusion.65
  29.1 1.2 fusion.67
  30.3 0.3 fusion.68
  30.6 0.6 fusion.69
  31.2 0.5 fusion.71
  31.7 1.5 bitcast_dynamic-update-slice_fusion.2
  33.1 0.5 fusion.70
  33.7 0.7 pad_maximum_fusion
  34.4 0.0 all-gather.2.cloned.1.call-update
  34.5 0.0 reduce-scatter.2.cloned.1.call-start
  34.5 19.3 %all-gather.2.cloned.1.call-done = bf16[512,1024]{1,0:T(8,128)(2,1)} async-done(((bf16[512,256]{1,0:T(8,128)(2,1)}), bf16[512,1024]{1,0:T(8,128)(2,1)}) %all-gather.2.cloned.1.call-update) | async-done | bytes 1048592 | tf_op jit(solution)/shard_map/all_gather | solution.py:78
  53.8 1.8 %reshape.32 = bf16[512,2,2,2,128]{4,3,2,1,0:T(2,128)(2,1)S(1)} reshape(bf16[512,1024]{1,0:T(8,128)(2,1)} %all-gather.2.cloned.1.call-done) | data formatting | bytes 2097152 | tf_op jit(solution)/shard_map/reshape | solution.py:81
  55.6 2.1 %reduce = bf16[512,2,2,128]{3,2,1,0:T(2,128)(2,1)S(1)} reduce(bf16[512,2,2,2,128]{4,3,2,1,0:T(2,128)(2,1)S(1)} %reshape.32, bf16[]{:T(256)} %constant.81.clone.1), dimensions={2}, to_apply=%region_5.6.clone | reduce | flops 262144 | bytes 1572866 | tf_op jit(solution)/shard_map/reduce_sum | solution.py:81
  57.8 0.2 convert_element_type.45
  58.0 6.5 %fusion.33 = bf16[4096,512]{0,1:T(8,128)(2,1)} fusion(bf16[512,512]{1,0:T(8,128)(2,1)S(1)} %convert_element_type.45, bf16[512,4096]{1,0:T(8,128)(2,1)} %param.7), kind=kOutput, calls=%fused_computation.42 | convolution fusion | flops 2151677952 | bytes 8912896 | tf_op jit(solution)/shard_map/dot_general | solution.py:92
  64.5 0.0 reduce-scatter.2.cloned.1.call-update
  64.5 2.9 %multiply_convert_fusion.1 = bf16[128,4,2,512]{3,0,2,1:T(8,128)(2,1)S(1)} fusion(bf16[4,2,512,512]{2,3,1,0:T(8,128)(2,1)} %get-tuple-element.159, bf16[512,128]{0,1:T(8,128)(2,1)S(1)} %get-tuple-element.242), kind=kOutput, calls=%fused_computation.43 | convolution fusion | flops 537919488 | bytes 5373952 | tf_op jit(solution)/shard_map/ghts,sd->tghd/dot_general | solution.py:87
  67.4 1.3 copy.32
  68.7 0.7 constant_dynamic-slice_fusion.1
  69.4 83.7 %reduce-scatter.2.cloned.1.call-done = bf16[512,512]{0,1:T(8,128)(2,1)} async-done(((bf16[4096,512]{0,1:T(8,128)(2,1)}), bf16[512,512]{0,1:T(8,128)(2,1)}) %reduce-scatter.2.cloned.1.call-update) | async-done | bytes 524304 | tf_op jit(solution)/shard_map/reduce_scatter | solution.py:95
  153.1 2.0 %copy.33 = bf16[512,512]{1,0:T(8,128)(2,1)} copy(bf16[512,512]{0,1:T(8,128)(2,1)} %reduce-scatter.2.cloned.1.call-done) | data formatting | bytes 1048576
  (10 shorter events, 0.2 us)
Async XLA Ops:
  7.2 46.7 %all-gather.2.cloned.1.call-start = ((), (), s32[]{:S(2)}) async-start(), calls=%async_computation.1 | async-start | bytes 1310720 | tf_op jit(solution)/shard_map/all_gather | solution.py:78
  8.2 3.5 %collective-permute-start = (bf16[512,128]{0,1:T(8,128)(2,1)S(1)}, bf16[512,128]{0,1:T(8,128)(2,1)S(1)}, u32[]{:S(2)}, u32[]{:S(2)}) collective-permute-start(bf16[512,128]{0,1:T(8,128)(2,1)S(1)} %copy.24), channel_id=1, source_target_pairs={{0,1},{1,0},{2,3},{3,2},{4,5},{5,4},{6,7},{7,6},{8,9},{9,8},{10,11... | collective-permute-start | bytes 393224 | tf_op jit(solution)/shard_map/ppermute | solution.py:10
  8.7 3.2 %copy-start = (s32[1,512]{1,0:T(1,128)S(1)}, s32[1,512]{1,0:T(1,128)}, u32[]{:S(2)}) copy-start(s32[1,512]{1,0:T(1,128)} %param.11) | copy-start | bytes 6148
  34.5 118.6 %reduce-scatter.2.cloned.1.call-start = ((), (), s32[]{:S(2)}) async-start(), calls=%async_computation.2 | async-start | bytes 4718592 | tf_op jit(solution)/shard_map/reduce_scatter | solution.py:95
Sparse Core Ops, SparseCore 0:
  34.6 19.2 all-gather.1
  64.6 88.4 reduce-scatter.1
where the time goes:
time: 162 us
  waiting for transfers between devices  103 us (64%)
  matrix products  23.2 us (14%)
  between operations  14.1 us (9%)
  local copies, waits for them, and re-layouts  10.9 us (7%)
  other arithmetic  9.78 us (6%)
    reduce_scatter x1, waiting for transfers between devices, shards(): lax.psum_scatter((product / sequences).astype(jnp.bfloat16), 'dp', scatte...  83.7 us
    all_gather x1, waiting for transfers between devices, shards(): lax.all_gather(stacked.astype(jnp.bfloat16), 'tensor', axis=1, tiled=True)  19.3 us
    unnamed x8, local copies, waits for them, and re-layouts  7.49 us
    dot_general x1, matrix products, shards(): lax.dot_general(layer_input, all_grads, (((0,), (0,)), ((), ())), preferr...  6.49 us
    dot_general x4, matrix products, score_block(): jnp.einsum('thd,sd->hts', grad_block, value_rows, preferred_element_type=...  5.95 us
    sub x4, other arithmetic, score_block(): weights = jnp.exp(scores - row_max)  4.83 us
  transfers between devices with their start and end apart: 3, of which 2 were waited for; matrix products, arithmetic and copies ran while one was open for 5% of the time, Pallas kernels for 0%

commit v1 on v0

--- a/solution.py
+++ b/solution.py
@@ -1,7 +1,394 @@
+import functools
+import math
 import jax
 import jax.numpy as jnp
 from jax import lax
+from jax.experimental import pallas as pl
+from jax.experimental.pallas import tpu as pltpu
 from jax.sharding import PartitionSpec as P
+
+F32 = jnp.float32
+BF16 = jnp.bfloat16
+
+
+def nt(a, b):
+    return lax.dot_general(a, b, (((1,), (1,)), ((), ())), preferred_element_type=F32)
+
+
+def nn(a, b):
+    return lax.dot_general(a, b, (((1,), (0,)), ((), ())), preferred_element_type=F32)
+
+
+def tn(a, b):
+    return lax.dot_general(a, b, (((0,), (0,)), ((), ())), preferred_element_type=F32)
+
+
+def kernel(
+    nd,
+    nt_dev,
+    feat,
+    li_hbm,
+    q_ref,
+    kv_ref,
+    og_ref,
+    seg_ref,
+    dq_ref,
+    gkv_ref,
+    gw_ref,
+    kv_in,
+    bias,
+    kt,
+    acc_k,
+    acc_v,
+    part_out,
+    part_in,
+    gbuf,
+    li,
+    pacc,
+    sbuf,
+    rbuf,
+    kv_sem,
+    lo_sem,
+    ls_sem,
+    lr_sem,
+    px_sem,
+    y_sem,
+    fwd_sem,
+    loc_sem,
+    xs_sem,
+    xr_sem,
+    cs_sem,
+    cr_sem,
+):
+    tok, hd = kv_ref.shape
+    heads = q_ref.shape[1] // hd
+    n = nd // 2
+    groups = nt_dev // 2
+    dp = lax.axis_index("dp")
+    te = lax.axis_index("tensor")
+    z = dp // 2
+    y = dp % 2
+    c = te % 2
+    grp = te // 2
+    other_y = z * 2 + 1 - y
+    mate = grp * 2 + 1 - c
+
+    def remote(src, dst, ssem, rsem, d, t):
+        return pltpu.make_async_remote_copy(
+            src_ref=src,
+            dst_ref=dst,
+            send_sem=ssem,
+            recv_sem=rsem,
+            device_id={"dp": d, "tensor": t},
+            device_id_type=pl.DeviceIdType.MESH,
+        )
+
+    barrier = pltpu.get_barrier_semaphore()
+    pl.semaphore_signal(
+        barrier, inc=1, device_id={"dp": other_y, "tensor": te}, device_id_type=pl.DeviceIdType.MESH
+    )
+    for step in (1, n - 1):
+        pl.semaphore_signal(
+            barrier,
+            inc=1,
+            device_id={"dp": ((z + step) % n) * 2 + y, "tensor": te},
+            device_id_type=pl.DeviceIdType.MESH,
+        )
+    for step in range(1, nt_dev):
+        pl.semaphore_signal(
+            barrier,
+            inc=1,
+            device_id={"dp": dp, "tensor": (te + step) % nt_dev},
+            device_id_type=pl.DeviceIdType.MESH,
+        )
+    pl.semaphore_wait(barrier, 3 + nt_dev - 1)
+
+    kv_copy = remote(kv_ref, kv_in, kv_sem.at[0], kv_sem.at[1], dp, mate)
+    kv_copy.start()
+
+    def feat_at(zz, yy):
+        return li_hbm.at[:, pl.ds(pl.multiple_of((zz * 2 + yy) * feat, feat), feat)]
+
+    def li_remote(zz):
+        return remote(
+            feat_at(zz, 1 - y),
+            li.at[zz, pl.ds(tok, tok), :],
+            ls_sem.at[zz],
+            lr_sem.at[zz],
+            other_y,
+            te,
+        )
+
+    def li_local(zz):
+        return pltpu.make_async_copy(feat_at(zz, y), li.at[zz, pl.ds(0, tok), :], lo_sem.at[zz])
+
+    def li_order(k):
+        low = n - 1 - k
+        low = jnp.where(low <= z, low - 1, low)
+        high = jnp.where(k >= z, k + 1, k)
+        v = jnp.where(z < n // 2, low, high)
+        return jnp.where(k == n - 1, z, v)
+
+    for k in range(n):
+        li_remote(li_order(k)).start()
+    for k in range(n):
+        li_local(k).start()
+
+    seg_b = jnp.broadcast_to(seg_ref[...].astype(F32), (tok, tok))
+    key_pos = lax.broadcasted_iota(jnp.int32, (tok, tok), 0)
+    qry_pos = lax.broadcasted_iota(jnp.int32, (tok, tok), 1)
+    allowed = (key_pos <= qry_pos) & (seg_b.T == seg_b)
+    bias[...] = jnp.where(allowed, 0.0, -1e30).astype(F32)
+    acc_k[...] = jnp.zeros_like(acc_k)
+    acc_v[...] = jnp.zeros_like(acc_v)
+    kv_copy.wait()
+    even = c == 0
+    keys = jnp.where(even, kv_ref[...], kv_in[...])
+    values = jnp.where(even, kv_in[...], kv_ref[...])
+    scale = hd**-0.5
+    coef = scale * math.log2(math.e)
+    kt[0] = keys
+    kt[1] = values
+    keys_t = keys.astype(F32).T.astype(BF16)
+    blk = tok // 2
+
+    def head(h, carry):
+        cols = pl.ds(pl.multiple_of(h * hd, hd), hd)
+        for b in range(2):
+            rows = pl.ds(b * blk, blk)
+            kc = (b + 1) * blk
+            q = q_ref[rows, cols]
+            o = og_ref[rows, cols]
+            s = nt(kt[0, 0:kc, :], q) * coef + bias[0:kc, rows]
+            m = jnp.max(s, axis=0, keepdims=True)
+            w = jnp.exp2(s - m)
+            inv = 1.0 / jnp.sum(w, axis=0, keepdims=True)
+            prob = w * inv
+            pb = prob.astype(BF16)
+            dpr = nt(kt[1, 0:kc, :], o)
+            delta = jnp.sum(pb.astype(F32) * dpr, axis=0, keepdims=True)
+            ds = (prob * (dpr - delta)).astype(BF16)
+            acc_v[0:kc, :] += nn(pb, o)
+            acc_k[0:kc, :] += nn(ds, q)
+            dqt = nn(keys_t[:, 0:kc], ds) * scale
+            dq_ref[rows, cols] = dqt.T.astype(BF16)
+        return carry
+
+    lax.fori_loop(0, heads, head, 0)
+
+    dk = acc_k[...] * scale
+    dv = acc_v[...]
+    part_out[...] = jnp.where(even, dv, dk).astype(BF16)
+    px = remote(part_out, part_in, px_sem.at[0], px_sem.at[1], dp, mate)
+    px.start()
+    mine = jnp.where(even, dk, dv)
+    px.wait()
+    gkv_ref[...] = (mine + part_in[...].astype(F32)).astype(BF16)
+
+    def cell(r, half, core):
+        lanes = pl.ds(pl.multiple_of(core * hd, hd), hd)
+        return gbuf.at[r, pl.ds(half * tok, tok), lanes]
+
+    own = pltpu.make_async_copy(gkv_ref, cell(0, 0, c), loc_sem)
+    own.start()
+    y_copy = remote(gkv_ref, cell(0, 1, c), y_sem.at[0], y_sem.at[1], other_y, te)
+    y_copy.start()
+    fwd0 = remote(gkv_ref, cell(0, 0, c), fwd_sem.at[0, 0], fwd_sem.at[1, 0], dp, mate)
+    fwd0.start()
+
+    def x_copy(r, core, half, src):
+        back = groups - r
+        return remote(
+            src,
+            cell(back, half, c),
+            xs_sem.at[r, core, half],
+            xr_sem.at[back, c, half],
+            dp,
+            ((grp + r) % groups) * 2 + core,
+        )
+
+    for r in range(1, groups):
+        for core in range(2):
+            x_copy(r, core, 0, gkv_ref).start()
+    y_copy.wait_recv()
+    fwd1 = remote(cell(0, 1, c), cell(0, 1, c), fwd_sem.at[0, 1], fwd_sem.at[1, 1], dp, mate)
+    fwd1.start()
+    for r in range(1, groups):
+        for core in range(2):
+            x_copy(r, core, 1, cell(0, 1, c)).start()
+    own.wait()
+    y_copy.wait_send()
+    for half, copy in ((0, fwd0), (1, fwd1)):
+        copy.wait_send()
+        land = cell(0, half, 1 - c)
+        remote(land, land, fwd_sem.at[0, half], fwd_sem.at[1, half], dp, mate).wait_recv()
+
+    inv_seq = 1.0 / nd
+
+    def product(r, zz):
+        pacc[...] = tn(li[zz], gbuf[r]) * inv_seq
+
+    def chain(side, r, zz):
+        step = 1 if side == 0 else -1
+        return remote(
+            sbuf.at[side, r, zz],
+            rbuf.at[side, r, zz],
+            cs_sem.at[side, r, zz],
+            cr_sem.at[side, r, zz],
+            (z + step) * 2 + y,
+            te,
+        )
+
+    def li_wait(zz):
+        li_local(zz).wait()
+        li_remote(zz).wait_recv()
+
+    def arrived(side, r, zz):
+        return remote(
+            sbuf.at[side, r, zz],
+            rbuf.at[side, r, zz],
+            cs_sem.at[side, r, zz],
+            cr_sem.at[side, r, zz],
+            ((z + 1) % n) * 2 + y,
+            te,
+        )
+
+    def hop(side, r, zz):
+        @pl.when(r == 0)
+        def _():
+            li_wait(zz)
+
+        product(r, zz)
+        inner = (z > 0) if side == 0 else (z < n - 1)
+
+        @pl.when(inner)
+        def _():
+            arrived(side, r, zz).wait_recv()
+            pacc[...] += rbuf[side, r, zz].astype(F32)
+
+        sbuf[side, r, zz] = pacc[...].astype(BF16)
+        chain(side, r, zz).start()
+
+    def group_step(r, carry):
+        @pl.when(r > 0)
+        def _():
+            for core in range(2):
+                for half in range(2):
+                    land = cell(r, half, core)
+                    remote(
+                        land, land, xs_sem.at[r, core, half], xr_sem.at[r, core, half], dp, mate
+                    ).wait_recv()
+
+        def dist_step(k, carry):
+            right = n - 1 - k
+
+            @pl.when(right > z)
+            def _():
+                hop(0, r, right)
+
+            @pl.when(k < z)
+            def _():
+                hop(1, r, k)
+
+            return carry
+
+        return lax.fori_loop(0, n - 1, dist_step, carry)
+
+    lax.fori_loop(0, groups, group_step, 0)
+    li_wait(z)
+
+    def finish(r, carry):
+        product(r, z)
+
+        @pl.when(z > 0)
+        def _():
+            arrived(0, r, z).wait_recv()
+            pacc[...] += rbuf[0, r, z].astype(F32)
+
+        @pl.when(z < n - 1)
+        def _():
+            arrived(1, r, z).wait_recv()
+            pacc[...] += rbuf[1, r, z].astype(F32)
+
+        width = 2 * hd
+        at = pl.multiple_of(((grp + r) % groups) * width, width)
+        gw_ref[:, pl.ds(at, width)] = pacc[...].astype(BF16)
+        return carry
+
+    lax.fori_loop(0, groups, finish, 0)
+
+    for k in range(n):
+        li_remote(k).wait_send()
+    for r in range(1, groups):
+        for core in range(2):
+            for half in range(2):
+                x_copy(r, core, half, cell(0, half, c)).wait_send()
+
+    def drain(r, carry):
+        def drain_step(k, carry):
+            right = n - 1 - k
+
+            @pl.when(right > z)
+            def _():
+                arrived(0, r, right).wait_send()
+
+            @pl.when(k < z)
+            def _():
+                arrived(1, r, k).wait_send()
+
+            return carry
+
+        return lax.fori_loop(0, n - 1, drain_step, carry)
+
+    lax.fori_loop(0, groups, drain, 0)
+
+
+def fused(nd, nt_dev, layer_input, queries, key_value, out_grad, segment_ids):
+    tok, hd = key_value.shape
+    feat = layer_input.shape[1] // nd
+    n, groups = nd // 2, nt_dev // 2
+    width = 2 * hd
+    vmem = pl.BlockSpec(memory_space=pltpu.VMEM)
+    dma = pltpu.SemaphoreType.DMA
+    return pl.pallas_call(
+        functools.partial(kernel, nd, nt_dev, feat),
+        out_shape=(
+            jax.ShapeDtypeStruct(queries.shape, BF16),
+            jax.ShapeDtypeStruct(key_value.shape, BF16),
+            jax.ShapeDtypeStruct((feat, width * groups), BF16),
+        ),
+        in_specs=[pl.BlockSpec(memory_space=pl.ANY), vmem, vmem, vmem, vmem],
+        out_specs=(vmem, vmem, vmem),
+        scratch_shapes=[
+            pltpu.VMEM((tok, hd), BF16),
+            pltpu.VMEM((tok, tok), F32),
+            pltpu.VMEM((2, tok, hd), BF16),
+            pltpu.VMEM((tok, hd), F32),
+            pltpu.VMEM((tok, hd), F32),
+            pltpu.VMEM((tok, hd), BF16),
+            pltpu.VMEM((tok, hd), BF16),
+            pltpu.VMEM((groups, 2 * tok, width), BF16),
+            pltpu.VMEM((n, 2 * tok, feat), BF16),
+            pltpu.VMEM((feat, width), F32),
+            pltpu.VMEM((2, groups, n, feat, width), BF16),
+            pltpu.VMEM((2, groups, n, feat, width), BF16),
+            dma((2,)),
+            dma((n,)),
+            dma((n,)),
+            dma((n,)),
+            dma((2,)),
+            dma((2,)),
+            dma((2, 2)),
+            dma,
+            dma((groups, 2, 2)),
+            dma((groups, 2, 2)),
+            dma((2, groups, n)),
+            dma((2, groups, n)),
+        ],
+        compiler_params=pltpu.CompilerParams(
+            collective_id=0, has_side_effects=True, vmem_limit_bytes=56 * 2**20
+        ),
+    )(layer_input, queries, key_value, out_grad, segment_ids)
 
 
 def partner_2(value, axis, stride):
@@ -99,8 +486,16 @@
 
 
 def solution(mesh):
+    nd, nt_dev = mesh.shape["dp"], mesh.shape["tensor"]
+
+    def body(layer_input, queries, key_value, out_grad, segment_ids):
+        feat = layer_input.shape[1] // nd
+        if feat % 128 or nd % 4 or nt_dev % 2:
+            return shards(layer_input, queries, key_value, out_grad, segment_ids)
+        return fused(nd, nt_dev, layer_input, queries, key_value, out_grad, segment_ids)
+
     return jax.shard_map(
-        shards,
+        body,
         mesh=mesh,
         in_specs=(
             P("dp", "tensor"),

time: 162 us -> 114 us (0.70)
  Pallas kernels: 0 us -> 108 us
  waiting for transfers between devices: 103 us -> 0 us
  matrix products: 23.2 us -> 0 us
  between operations: 14.1 us -> 0.64 us
  other arithmetic: 9.78 us -> 0 us
  local copies, waits for them, and re-layouts: 10.9 us -> 5.7 us
    pallas_call x0 -> x1, Pallas kernels: none -> 108 us  [fused(): pl.pallas_call(functools.partial(kernel, nd, nt_dev, feat), out_shape=(ja...]
    reduce_scatter x1 -> x0, waiting for transfers between devices: 83.7 us -> none  [shards(): lax.psum_scatter((product / sequences).astype(jnp.bfloat16), 'dp', scatte...]
    dot_general x22 -> x0, matrix products: 23.2 us -> none  [the longest x1 6.49 us: shards(): lax.dot_general(layer_input, all_grads, (((0,), (0,)), ((), ())), preferr...]
    all_gather x1 -> x0, waiting for transfers between devices: 19.3 us -> none  [shards(): lax.all_gather(stacked.astype(jnp.bfloat16), 'tensor', axis=1, tiled=True)]
    sub x4 -> x0, other arithmetic: 4.83 us -> none  [score_block(): weights = jnp.exp(scores - row_max)]
    reduce_sum x1 -> x0, other arithmetic: 2.13 us -> none  [shards(): every_part.reshape(tok_rows, tensor_count // 2, 2, 2, head_width)]
    unnamed x8 -> x3, local copies, waits for them, and re-layouts: 7.49 us -> 5.7 us
    reshape x1 -> x0, local copies, waits for them, and re-layouts: 1.79 us -> none  [shards(): every_part.reshape(tok_rows, tensor_count // 2, 2, 2, head_width)]
  transfers between devices with their start and end apart: 3 -> 0, of which waited for: 2 -> 0; matrix products, arithmetic and copies ran while one was open for 5% -> 0% of each run, Pallas kernels for 0% -> 0%
where the time goes in v1:
time: 114 us
  Pallas kernels  108 us (95%)
  local copies, waits for them, and re-layouts  5.7 us (5%)
    pallas_call x1, Pallas kernels, fused(): pl.pallas_call(functools.partial(kernel, nd, nt_dev, feat), out_shape=(ja...  108 us
    unnamed x3, local copies, waits for them, and re-layouts  5.7 us

profile of v1, /device:TPU:0, one launch (start us, length us, event | category | flops | bytes accessed | tf_op | source)
XLA Modules:
  0.0 114.1 jit_solution(4112875460611584233)
XLA Ops:
  0.6 107.7 %shard_map.76 = (bf16[512,1024]{1,0:T(8,128)(2,1)}, bf16[512,128]{1,0:T(8,128)(2,1)}, bf16[512,512]{1,0:T(8,128)(2,1)}) custom-call(bf16[512,4096]{1,0:T(8,128)(2,1)} %li_hbm.1, bf16[512,1024]{1,0:T(8,128)(2,1)} %q_ref.1, bf16[512,128]{1,0:T(8,128)(2,1)} %kv_ref.1, bf16[512,1024]{1,0:T(8,128)(2,1)} %og_ref.1, s32[1,512]{1,0:T(1,128)} %seg_ref.1), custom_call_target="tpu_custom_call" | custom-call | tf_op jit(solution)/shard_map/pallas_call | solution.py:353
  108.4 2.3 %copy.11 = bf16[512,1024]{1,0:T(8,128)(2,1)} copy(bf16[512,1024]{1,0:T(8,128)(2,1)} %get-tuple-element.6) | data formatting | bytes 2097152
  110.6 1.6 %copy.12 = bf16[512,128]{1,0:T(8,128)(2,1)} copy(bf16[512,128]{1,0:T(8,128)(2,1)} %get-tuple-element.7) | data formatting | bytes 262144
  112.2 1.9 %copy.13 = bf16[512,512]{1,0:T(8,128)(2,1)} copy(bf16[512,512]{1,0:T(8,128)(2,1)} %get-tuple-element.8) | data formatting | bytes 1048576

commit v2 on v1

--- a/solution.py
+++ b/solution.py
@@ -129,8 +129,7 @@
         v = jnp.where(z < n // 2, low, high)
         return jnp.where(k == n - 1, z, v)
 
-    for k in range(n):
-        li_remote(li_order(k)).start()
+    li_remote(li_order(0)).start()
     for k in range(n):
         li_local(k).start()
 
@@ -176,6 +175,11 @@
 
     lax.fori_loop(0, heads, head, 0)
 
+    def li_next(k):
+        li_remote(li_order(k - 1)).wait_send()
+        li_remote(li_order(k)).start()
+
+    li_next(1)
     dk = acc_k[...] * scale
     dv = acc_v[...]
     part_out[...] = jnp.where(even, dv, dk).astype(BF16)
@@ -254,10 +258,6 @@
         )
 
     def hop(side, r, zz):
-        @pl.when(r == 0)
-        def _():
-            li_wait(zz)
-
         product(r, zz)
         inner = (z > 0) if side == 0 else (z < n - 1)
 
@@ -269,32 +269,38 @@
         sbuf[side, r, zz] = pacc[...].astype(BF16)
         chain(side, r, zz).start()
 
-    def group_step(r, carry):
-        @pl.when(r > 0)
+    def dist_step(k, carry):
+        zz = li_order(k)
+        li_wait(zz)
+
+        @pl.when(k < n - 2)
         def _():
-            for core in range(2):
-                for half in range(2):
-                    land = cell(r, half, core)
-                    remote(
-                        land, land, xs_sem.at[r, core, half], xr_sem.at[r, core, half], dp, mate
-                    ).wait_recv()
-
-        def dist_step(k, carry):
-            right = n - 1 - k
-
-            @pl.when(right > z)
+            li_next(k + 2)
+
+        def group_step(r, carry):
+            @pl.when((k == 0) & (r > 0))
             def _():
-                hop(0, r, right)
-
-            @pl.when(k < z)
+                for core in range(2):
+                    for half in range(2):
+                        land = cell(r, half, core)
+                        remote(
+                            land, land, xs_sem.at[r, core, half], xr_sem.at[r, core, half], dp, mate
+                        ).wait_recv()
+
+            @pl.when(zz > z)
             def _():
-                hop(1, r, k)
+                hop(0, r, zz)
+
+            @pl.when(zz < z)
+            def _():
+                hop(1, r, zz)
 
             return carry
 
-        return lax.fori_loop(0, n - 1, dist_step, carry)
-
-    lax.fori_loop(0, groups, group_step, 0)
+        return lax.fori_loop(0, groups, group_step, carry)
+
+    lax.fori_loop(0, n - 1, dist_step, 0)
+
     li_wait(z)
 
     def finish(r, carry):
@@ -317,8 +323,7 @@
 
     lax.fori_loop(0, groups, finish, 0)
 
-    for k in range(n):
-        li_remote(k).wait_send()
+    li_remote(z).wait_send()
     for r in range(1, groups):
         for core in range(2):
             for half in range(2):

time: 114 us -> 83.2 us (0.73)
  Pallas kernels: 108 us -> 76.6 us
    pallas_call x1, Pallas kernels: 108 us -> 76.6 us  [fused(): pl.pallas_call(functools.partial(kernel, nd, nt_dev, feat), out_shape=(ja...]
where the time goes in v2:
time: 83.2 us; the launch traced here: 82.9 us
  Pallas kernels  76.6 us (92%)
  local copies, waits for them, and re-layouts  5.7 us (7%)
    pallas_call x1, Pallas kernels, fused(): pl.pallas_call(functools.partial(kernel, nd, nt_dev, feat), out_shape=(ja...  76.6 us
    unnamed x3, local copies, waits for them, and re-layouts  5.7 us

profile of v2, /device:TPU:0, one launch (start us, length us, event | category | flops | bytes accessed | tf_op | source)
XLA Modules:
  0.0 82.9 jit_solution(9900349346946196889)
XLA Ops:
  0.6 76.6 %shard_map.76 = (bf16[512,1024]{1,0:T(8,128)(2,1)}, bf16[512,128]{1,0:T(8,128)(2,1)}, bf16[512,512]{1,0:T(8,128)(2,1)}) custom-call(bf16[512,4096]{1,0:T(8,128)(2,1)} %li_hbm.1, bf16[512,1024]{1,0:T(8,128)(2,1)} %q_ref.1, bf16[512,128]{1,0:T(8,128)(2,1)} %kv_ref.1, bf16[512,1024]{1,0:T(8,128)(2,1)} %og_ref.1, s32[1,512]{1,0:T(1,128)} %seg_ref.1), custom_call_target="tpu_custom_call" | custom-call | tf_op jit(solution)/shard_map/pallas_call | solution.py:358
  77.2 2.3 %copy.11 = bf16[512,1024]{1,0:T(8,128)(2,1)} copy(bf16[512,1024]{1,0:T(8,128)(2,1)} %get-tuple-element.6) | data formatting | bytes 2097152
  79.5 1.6 %copy.12 = bf16[512,128]{1,0:T(8,128)(2,1)} copy(bf16[512,128]{1,0:T(8,128)(2,1)} %get-tuple-element.7) | data formatting | bytes 262144
  81.0 1.9 %copy.13 = bf16[512,512]{1,0:T(8,128)(2,1)} copy(bf16[512,512]{1,0:T(8,128)(2,1)} %get-tuple-element.8) | data formatting | bytes 1048576

commit v3 on v2

--- a/solution.py
+++ b/solution.py
@@ -490,6 +490,29 @@
     return (grad_query, grad_pair, weight_grad)
 
 
+def move(*refs):
+    count = (len(refs) - 1) // 2
+    sem = refs[-1]
+    copies = [
+        pltpu.make_async_copy(refs[i], refs[count + i], sem.at[i]) for i in range(count)
+    ]
+    for copy in copies:
+        copy.start()
+    for copy in copies:
+        copy.wait()
+
+
+def settle(results):
+    anywhere = pl.BlockSpec(memory_space=pl.ANY)
+    return pl.pallas_call(
+        move,
+        out_shape=tuple(jax.ShapeDtypeStruct(v.shape, v.dtype) for v in results),
+        in_specs=[pl.BlockSpec(memory_space=pltpu.VMEM)] * len(results),
+        out_specs=(anywhere,) * len(results),
+        scratch_shapes=[pltpu.SemaphoreType.DMA((len(results),))],
+    )(*results)
+
+
 def solution(mesh):
     nd, nt_dev = mesh.shape["dp"], mesh.shape["tensor"]
 
@@ -497,7 +520,7 @@
         feat = layer_input.shape[1] // nd
         if feat % 128 or nd % 4 or nt_dev % 2:
             return shards(layer_input, queries, key_value, out_grad, segment_ids)
-        return fused(nd, nt_dev, layer_input, queries, key_value, out_grad, segment_ids)
+        return settle(fused(nd, nt_dev, layer_input, queries, key_value, out_grad, segment_ids))
 
     return jax.shard_map(
         body,

time: 83.2 us -> 80 us (0.962)
  local copies, waits for them, and re-layouts: 5.7 us -> 0 us
  Pallas kernels: 76.6 us -> 79.2 us
    unnamed x3 -> x0, local copies, waits for them, and re-layouts: 5.7 us -> none
    pallas_call x0 -> x1, Pallas kernels: none -> 2.64 us  [settle(): pl.pallas_call(move, out_shape=tuple((jax.ShapeDtypeStruct(v.shape, v.dty...]
where the time goes in v3:
time: 80 us; the launch traced here: 79.8 us
  Pallas kernels  79.2 us (99%)
    pallas_call x1, Pallas kernels, fused(): pl.pallas_call(functools.partial(kernel, nd, nt_dev, feat), out_shape=(ja...  76.6 us
    pallas_call x1, Pallas kernels, settle(): pl.pallas_call(move, out_shape=tuple((jax.ShapeDtypeStruct(v.shape, v.dty...  2.64 us

profile of v3, /device:TPU:0, one launch (start us, length us, event | category | flops | bytes accessed | tf_op | source)
XLA Modules:
  0.0 79.8 jit_solution(3759889688980766856)
XLA Ops:
  0.6 76.6 %shard_map.76 = (bf16[512,1024]{1,0:T(8,128)(2,1)}, bf16[512,128]{1,0:T(8,128)(2,1)}, bf16[512,512]{1,0:T(8,128)(2,1)}) custom-call(bf16[512,4096]{1,0:T(8,128)(2,1)} %li_hbm.1, bf16[512,1024]{1,0:T(8,128)(2,1)} %q_ref.1, bf16[512,128]{1,0:T(8,128)(2,1)} %kv_ref.1, bf16[512,1024]{1,0:T(8,128)(2,1)} %og_ref.1, s32[1,512]{1,0:T(1,128)} %seg_ref.1), custom_call_target="tpu_custom_call" | custom-call | tf_op jit(solution)/shard_map/pallas_call | solution.py:358
  77.2 2.6 %shard_map.77 = (bf16[512,1024]{1,0:T(8,128)(2,1)}, bf16[512,128]{1,0:T(8,128)(2,1)}, bf16[512,512]{1,0:T(8,128)(2,1)}) custom-call(bf16[512,1024]{1,0:T(8,128)(2,1)} %get-tuple-element.6.refs_0_, bf16[512,128]{1,0:T(8,128)(2,1)} %get-tuple-element.7.refs_1_, bf16[512,512]{1,0:T(8,128)(2,1)} %get-tuple-element.8.refs_2_), custom_call_target="tpu_custom_call" | custom-call | tf_op jit(solution)/shard_map/pallas_call | solution.py:507
